TPU v7x, 256 devices: a whole 4x4x8 slice. The times are simulated.
256 devices in a mesh: section: 8 (over z), lon: 32 (over y, x, core).
Axes of the slice: x: 4, y: 4, z: 8, core: 2. Of those that a mesh axis runs over, the one named last changes fastest.
Arguments:
- lanczos_block: bfloat16 [16, 8, 256, 512], P(None, None, 'lon'), may hold values from -9 to 9
- previous: bfloat16 [16, 8, 256, 512], P(None, 'section', 'lon'), may hold values from -6 to 6
- beta_prev: float32 [16, 16], replicated, may hold values from -2 to 2, as said below
- weights: bfloat16 [8, 9, 512, 512], P('section'), may hold values from -0.09375 to 0.09375
- act_slope: bfloat16 [8, 8, 256, 512], P('section', None, 'lon'), may hold values from 0 to 1.09375
- metric: float32 [8, 256], P(None, 'lon'), may hold values from 0.3 to 3
Outputs:
- residual_block: float32 [16, 8, 256, 512], P(None, 'section', 'lon')
- projection: float32 [16, 16], replicated
- residual_gram: float32 [16, 16], replicated
Inputs may be any that keep to these rules, and one draw needn't show every extreme that they name: `beta_prev`: upper triangular, with a positive diagonal.
All inputs are finite; a program needn't handle non-finite values.
Results may differ from a plain program's by a relative error of at most 0.02.
Values may be sent and summed in bfloat16 or wider, within the bound.
No kernel may reach another device: no remote copies, remote signals or barrier semaphores. Data moves between devices by JAX's collectives and lax.ppermute only.
A program may use at most 64 MiB of HBM per device.

v0:
```python
import jax
import jax.numpy as jnp
from jax import lax
from jax.sharding import PartitionSpec as P

K = 16
DILATION_SIZE = 4


def padded(cells, sides, width):
    for axis, dim in sides:
        count = lax.axis_size(axis)
        head = lax.slice_in_dim(cells, 0, width, axis=dim)
        tail = lax.slice_in_dim(cells, cells.shape[dim] - width, cells.shape[dim], axis=dim)
        cells = jnp.concatenate(
            [
                lax.ppermute(tail, axis, [(i, (i + 1) % count) for i in range(count)]),
                cells,
                lax.ppermute(head, axis, [((i + 1) % count, i) for i in range(count)]),
            ],
            axis=dim,
        )
    return cells


def from_behind(shard, axis, by):
    count = lax.axis_size(axis)
    pairs = [(i, i + by) for i in range(count) if 0 <= i + by < count]
    return lax.ppermute(shard, axis, pairs)


def broadcast(shard, axis, root):
    mine = lax.axis_index(axis) == root
    return lax.psum(jnp.where(mine, shard, jnp.zeros_like(shard)), axis)


def spread_taps(input_field, tap_weights, direction_sign, border_width):
    micro_size = input_field.shape[0]
    lat_rows = input_field.shape[1]
    lon_cols = input_field.shape[2] - 2 * border_width
    channels = input_field.shape[3]
    padded_field = jnp.pad(input_field, ((0, 0), (border_width, border_width), (0, 0), (0, 0)))
    summed = jnp.zeros((micro_size * lat_rows * lon_cols, channels), jnp.float32)
    for row_stride in (-1, 0, 1):
        for column_stride in (-1, 0, 1):
            tap_index = 3 * (row_stride + 1) + (column_stride + 1)
            first_row = border_width + direction_sign * row_stride * border_width
            col_start = border_width + direction_sign * column_stride * border_width
            tap_rows = padded_field[
                :, first_row : first_row + lat_rows, col_start : col_start + lon_cols, :
            ].reshape(-1, channels)
            if direction_sign > 0:
                summed = summed + jnp.dot(
                    tap_rows, tap_weights[tap_index], preferred_element_type=jnp.float32
                )
            else:
                summed = summed + lax.dot_general(
                    tap_rows,
                    tap_weights[tap_index],
                    (((1,), (1,)), ((), ())),
                    preferred_element_type=jnp.float32,
                )
    return summed.reshape(micro_size, lat_rows, lon_cols, channels)


def body(lanczos_block, previous, beta_prev, weights, act_slope, metric):
    section_count = lax.axis_size("section")
    section_index = lax.axis_index("section")
    tap_weights = weights[0]
    slope_here = act_slope[0].astype(jnp.float32)[None]
    border_width = DILATION_SIZE
    micro_count = 2
    micro_size = K // micro_count
    slot_shape = (micro_size,) + lanczos_block.shape[1:]
    lon_cols = lanczos_block.shape[2]
    micro_feeds = lanczos_block.reshape((micro_count,) + slot_shape)
    tick_count = micro_count + section_count - 1
    zero_slot = jnp.zeros(slot_shape, jnp.bfloat16)
    empty_store = jnp.zeros((micro_count,) + slot_shape, jnp.bfloat16)

    def forward_layer(rimmed):
        convolved = spread_taps(rimmed, tap_weights, 1, border_width)
        centre = rimmed[:, :, border_width : border_width + lon_cols, :].astype(jnp.float32)
        return (centre + slope_here * convolved).astype(jnp.bfloat16)

    def skip_forward(rimmed):
        return zero_slot

    def forward_tick(state_pair, tick_now):
        inbound, forward_out = state_pair
        micro_index = tick_now - section_index
        active = (micro_index >= 0) & (micro_index < micro_count)
        slot_index = jnp.clip(micro_index, 0, micro_count - 1)
        fed_slot = lax.dynamic_index_in_dim(micro_feeds, slot_index, 0, keepdims=False)
        incoming = jnp.where(section_index == 0, fed_slot, inbound)
        rimmed = padded(incoming, (("lon", 2),), border_width)
        result = lax.cond(active, forward_layer, skip_forward, rimmed)
        keep_slot = active & (section_index == section_count - 1)
        old_slot = lax.dynamic_index_in_dim(forward_out, slot_index, 0, keepdims=False)
        forward_out = lax.dynamic_update_index_in_dim(
            forward_out, jnp.where(keep_slot, result, old_slot), slot_index, 0
        )
        outbound = from_behind(result, "section", 1)
        return ((outbound, forward_out), None)

    (unused_slot, forward_out), unused_out = lax.scan(
        forward_tick, (zero_slot, empty_store), jnp.arange(tick_count, dtype=jnp.int32)
    )
    metric_here = metric[None, :, :, None]

    def backward_layer(operands):
        incoming, rimmed = operands
        convolved = spread_taps(rimmed, tap_weights, -1, border_width)
        return (incoming.astype(jnp.float32) + convolved).astype(jnp.bfloat16)

    def skip_backward(operands):
        return zero_slot

    def backward_tick(state_pair, tick_now):
        inbound, adjoint_out = state_pair
        micro_index = tick_now - (section_count - 1 - section_index)
        active = (micro_index >= 0) & (micro_index < micro_count)
        slot_index = jnp.clip(micro_index, 0, micro_count - 1)
        stored_slot = lax.dynamic_index_in_dim(forward_out, slot_index, 0, keepdims=False)
        started = (metric_here * stored_slot.astype(jnp.float32)).astype(jnp.bfloat16)
        incoming = jnp.where(section_index == section_count - 1, started, inbound)
        sensitivity = (slope_here * incoming.astype(jnp.float32)).astype(jnp.bfloat16)
        rimmed = padded(sensitivity, (("lon", 2),), border_width)
        result = lax.cond(active, backward_layer, skip_backward, (incoming, rimmed))
        keep_slot = active & (section_index == 0)
        old_slot = lax.dynamic_index_in_dim(adjoint_out, slot_index, 0, keepdims=False)
        adjoint_out = lax.dynamic_update_index_in_dim(
            adjoint_out, jnp.where(keep_slot, result, old_slot), slot_index, 0
        )
        outbound = from_behind(result, "section", -1)
        return ((outbound, adjoint_out), None)

    (unused_back, adjoint_out), unused_more = lax.scan(
        backward_tick, (zero_slot, empty_store), jnp.arange(tick_count, dtype=jnp.int32)
    )
    applied = adjoint_out.reshape(lanczos_block.shape)
    applied_all = broadcast(applied, "section", 0)
    row_count = previous.shape[1]
    applied_rows = lax.dynamic_slice_in_dim(applied_all, section_index * row_count, row_count, 1)
    own_block = lax.dynamic_slice_in_dim(lanczos_block, section_index * row_count, row_count, 1)
    high = lax.Precision.HIGHEST
    cell_count = (
        lanczos_block.shape[1]
        * lanczos_block.shape[2]
        * lax.axis_size("lon")
        * lanczos_block.shape[3]
    )
    block_flat = own_block.reshape(K, -1).astype(jnp.float32)
    prev_flat = previous.reshape(K, -1).astype(jnp.float32)
    shifted = applied_rows.reshape(K, -1).astype(jnp.float32) - jnp.dot(
        beta_prev, prev_flat, precision=high
    )
    part_projection = jnp.dot(block_flat, shifted.T, precision=high) / cell_count
    projection = lax.psum(part_projection, ("section", "lon"))
    residual_rows = shifted - jnp.dot(projection.T, block_flat, precision=high)
    part_gram = jnp.dot(residual_rows, residual_rows.T, precision=high) / cell_count
    residual_gram = lax.psum(part_gram, ("section", "lon"))
    return (residual_rows.reshape(own_block.shape), projection, residual_gram)


def solution(mesh):
    return jax.shard_map(
        body,
        mesh=mesh,
        in_specs=(
            P(None, None, "lon", None),
            P(None, "section", "lon", None),
            P(),
            P("section", None, None, None),
            P("section", None, "lon", None),
            P(None, "lon"),
        ),
        out_specs=(P(None, "section", "lon", None), P(), P()),
        check_vma=False,
    )
```

profile of v0, /device:TPU:1, one launch (start us, length us, event | category | flops | bytes accessed | tf_op | source)
XLA Modules:
  0.0 797.1 jit_solution(21797135074578725)
XLA Ops:
  8.3 248.3 %while.27 = (s32[]{:T(128)}, bf16[8,8,8,512]{3,2,1,0:T(8,128)(2,1)S(1)}, bf16[2,8,8,8,512]{4,3,2,1,0:T(8,128)(2,1)S(1)}, s32[9]{0:T(128)S(1)}, s32[]{:T(128)}, /...) while((s32[]{:T(128)}, ...), condition=%wide.region_3.4_spmd, body=%wide.region_0.3_spmd.sunk | while | flops 2422734848 | bytes 67240344 | solution.py:106
  10.8 3.3 collective-permute-start
  14.0 3.4 collective-permute-done
  18.7 6.5 conditional.4
  26.8 5.8 collective-permute-done.2
  35.1 8.7 %collective-permute-start = (bf16[8,8,4,512]{3,2,1,0:T(4,128)(2,1)S(1)}, bf16[8,8,4,512]{3,2,1,0:T(4,128)(2,1)S(1)}, u32[]{:S(2)}, u32[]{:S(2)}) collective-permute-start(bf16[8,8,4,512]{3,2,1,0:T(4,128)(2,1)S(1)} %get-tuple-element.424), channel_id=1, source_target_pairs={{1,0},{2,1},{3,2},{4,3},{5,4},{6,5},{7,6},{8,7},{9,8},{10,9},{11,1... | collective-permute-start | bytes 786440 | tf_op jit(solution)/shard_map/while/body/eval_jaxpr/ppermute | solution.py:19
  43.8 2.3 collective-permute-done
  48.4 6.5 conditional.4
  54.9 3.8 collective-permute-start.2
  59.0 5.8 collective-permute-done.2
  67.3 9.0 %collective-permute-start = (bf16[8,8,4,512]{3,2,1,0:T(4,128)(2,1)S(1)}, bf16[8,8,4,512]{3,2,1,0:T(4,128)(2,1)S(1)}, u32[]{:S(2)}, u32[]{:S(2)}) collective-permute-start(bf16[8,8,4,512]{3,2,1,0:T(4,128)(2,1)S(1)} %get-tuple-element.424), channel_id=1, source_target_pairs={{1,0},{2,1},{3,2},{4,3},{5,4},{6,5},{7,6},{8,7},{9,8},{10,9},{11,1... | collective-permute-start | bytes 786440 | tf_op jit(solution)/shard_map/while/body/eval_jaxpr/ppermute | solution.py:19
  77.5 2.1 collective-permute-done.1
  80.4 10.6 %collective-permute-start.2 = (bf16[8,8,8,512]{3,2,1,0:T(8,128)(2,1)S(1)}, bf16[8,8,8,512]{3,2,1,0:T(8,128)(2,1)S(1)}, u32[]{:S(2)}, u32[]{:S(2)}) collective-permute-start(bf16[8,8,8,512]{3,2,1,0:T(8,128)(2,1)S(1)} %get-tuple-element.522), channel_id=1, source_target_pairs={{0,32},{32,64},{64,96},{96,128},{128,160},{160,192},{192,224},{1,3... | collective-permute-start | bytes 1572872 | tf_op jit(solution)/shard_map/while/body/eval_jaxpr/ppermute | solution.py:29
  91.2 5.8 collective-permute-done.2
  99.6 8.1 %collective-permute-start = (bf16[8,8,4,512]{3,2,1,0:T(4,128)(2,1)S(1)}, bf16[8,8,4,512]{3,2,1,0:T(4,128)(2,1)S(1)}, u32[]{:S(2)}, u32[]{:S(2)}) collective-permute-start(bf16[8,8,4,512]{3,2,1,0:T(4,128)(2,1)S(1)} %get-tuple-element.424), channel_id=1, source_target_pairs={{1,0},{2,1},{3,2},{4,3},{5,4},{6,5},{7,6},{8,7},{9,8},{10,9},{11,1... | collective-permute-start | bytes 786440 | tf_op jit(solution)/shard_map/while/body/eval_jaxpr/ppermute | solution.py:19
  108.8 2.2 collective-permute-done.1
  111.7 4.1 collective-permute-start.2
  116.1 5.8 collective-permute-done.2
  124.4 7.2 collective-permute-start
  132.8 2.2 collective-permute-done.1
  135.7 8.7 %collective-permute-start.2 = (bf16[8,8,8,512]{3,2,1,0:T(8,128)(2,1)S(1)}, bf16[8,8,8,512]{3,2,1,0:T(8,128)(2,1)S(1)}, u32[]{:S(2)}, u32[]{:S(2)}) collective-permute-start(bf16[8,8,8,512]{3,2,1,0:T(8,128)(2,1)S(1)} %get-tuple-element.522), channel_id=1, source_target_pairs={{0,32},{32,64},{64,96},{96,128},{128,160},{160,192},{192,224},{1,3... | collective-permute-start | bytes 1572872 | tf_op jit(solution)/shard_map/while/body/eval_jaxpr/ppermute | solution.py:29
  144.6 5.8 collective-permute-done.2
  152.9 7.4 collective-permute-start
  161.5 2.2 collective-permute-done.1
  164.4 4.1 collective-permute-start.2
  168.8 5.8 collective-permute-done.2
  177.1 6.8 collective-permute-start
  185.1 2.2 collective-permute-done.1
  188.0 8.7 %collective-permute-start.2 = (bf16[8,8,8,512]{3,2,1,0:T(8,128)(2,1)S(1)}, bf16[8,8,8,512]{3,2,1,0:T(8,128)(2,1)S(1)}, u32[]{:S(2)}, u32[]{:S(2)}) collective-permute-start(bf16[8,8,8,512]{3,2,1,0:T(8,128)(2,1)S(1)} %get-tuple-element.522), channel_id=1, source_target_pairs={{0,32},{32,64},{64,96},{96,128},{128,160},{160,192},{192,224},{1,3... | collective-permute-start | bytes 1572872 | tf_op jit(solution)/shard_map/while/body/eval_jaxpr/ppermute | solution.py:29
  196.9 5.8 collective-permute-done.2
  205.2 6.8 collective-permute-start
  213.2 2.2 collective-permute-done.1
  216.1 4.1 collective-permute-start.2
  220.5 5.8 collective-permute-done.2
  228.8 6.8 collective-permute-start
  236.8 2.2 collective-permute-done.1
  239.7 10.7 %collective-permute-start.2 = (bf16[8,8,8,512]{3,2,1,0:T(8,128)(2,1)S(1)}, bf16[8,8,8,512]{3,2,1,0:T(8,128)(2,1)S(1)}, u32[]{:S(2)}, u32[]{:S(2)}) collective-permute-start(bf16[8,8,8,512]{3,2,1,0:T(8,128)(2,1)S(1)} %get-tuple-element.522), channel_id=1, source_target_pairs={{0,32},{32,64},{64,96},{96,128},{128,160},{160,192},{192,224},{1,3... | collective-permute-start | bytes 1572872 | tf_op jit(solution)/shard_map/while/body/eval_jaxpr/ppermute | solution.py:29
  250.7 5.8 collective-permute-done.2
  257.5 306.7 %while.28 = (s32[]{:T(128)}, bf16[8,8,8,512]{3,2,1,0:T(8,128)(2,1)}, bf16[2,8,8,8,512]{4,3,2,1,0:T(8,128)(2,1)S(1)}, s32[9]{0:T(128)S(1)}, s32[]{:T(128)}, /*ind...) while((s32[]{:T(128)}, ...), condition=%wide.region_7.8_spmd, body=%wide.region_4.7_spmd.sunk | while | flops 2424045568 | bytes 67764888 | solution.py:138
  261.0 6.7 collective-permute-start.3
  274.4 10.3 %collective-permute-done.5 = bf16[8,8,8,512]{3,2,1,0:T(8,128)(2,1)} collective-permute-done((bf16[8,8,8,512]{3,2,1,0:T(8,128)(2,1)S(1)}, bf16[8,8,8,512]{3,2,1,0:T(8,128)(2,1)}, u32[]{:S(2)}, u32[]{:S(2)}) %collective-permute-start.5) | collective-permute-done | bytes 524320 | tf_op jit(solution)/shard_map/while/body/eval_jaxpr/ppermute | solution.py:29
  288.2 6.8 collective-permute-start.3
  301.6 12.0 %collective-permute-done.5 = bf16[8,8,8,512]{3,2,1,0:T(8,128)(2,1)} collective-permute-done((bf16[8,8,8,512]{3,2,1,0:T(8,128)(2,1)S(1)}, bf16[8,8,8,512]{3,2,1,0:T(8,128)(2,1)}, u32[]{:S(2)}, u32[]{:S(2)}) %collective-permute-start.5) | collective-permute-done | bytes 524320 | tf_op jit(solution)/shard_map/while/body/eval_jaxpr/ppermute | solution.py:29
  317.2 6.8 collective-permute-start.3
  330.6 10.5 %collective-permute-done.5 = bf16[8,8,8,512]{3,2,1,0:T(8,128)(2,1)} collective-permute-done((bf16[8,8,8,512]{3,2,1,0:T(8,128)(2,1)S(1)}, bf16[8,8,8,512]{3,2,1,0:T(8,128)(2,1)}, u32[]{:S(2)}, u32[]{:S(2)}) %collective-permute-start.5) | collective-permute-done | bytes 524320 | tf_op jit(solution)/shard_map/while/body/eval_jaxpr/ppermute | solution.py:29
  344.6 6.8 collective-permute-start.3
  358.0 12.0 %collective-permute-done.5 = bf16[8,8,8,512]{3,2,1,0:T(8,128)(2,1)} collective-permute-done((bf16[8,8,8,512]{3,2,1,0:T(8,128)(2,1)S(1)}, bf16[8,8,8,512]{3,2,1,0:T(8,128)(2,1)}, u32[]{:S(2)}, u32[]{:S(2)}) %collective-permute-start.5) | collective-permute-done | bytes 524320 | tf_op jit(solution)/shard_map/while/body/eval_jaxpr/ppermute | solution.py:29
  373.6 6.8 collective-permute-start.3
  381.8 1.8 collective-permute-done.4
  386.9 10.0 %collective-permute-done.5 = bf16[8,8,8,512]{3,2,1,0:T(8,128)(2,1)} collective-permute-done((bf16[8,8,8,512]{3,2,1,0:T(8,128)(2,1)S(1)}, bf16[8,8,8,512]{3,2,1,0:T(8,128)(2,1)}, u32[]{:S(2)}, u32[]{:S(2)}) %collective-permute-start.5) | collective-permute-done | bytes 524320 | tf_op jit(solution)/shard_map/while/body/eval_jaxpr/ppermute | solution.py:29
  400.5 6.8 collective-permute-start.3
  413.9 12.5 %collective-permute-done.5 = bf16[8,8,8,512]{3,2,1,0:T(8,128)(2,1)} collective-permute-done((bf16[8,8,8,512]{3,2,1,0:T(8,128)(2,1)S(1)}, bf16[8,8,8,512]{3,2,1,0:T(8,128)(2,1)}, u32[]{:S(2)}, u32[]{:S(2)}) %collective-permute-start.5) | collective-permute-done | bytes 524320 | tf_op jit(solution)/shard_map/while/body/eval_jaxpr/ppermute | solution.py:29
  429.9 6.8 collective-permute-start.3
  438.2 1.8 collective-permute-done.4
  443.3 54.9 %collective-permute-done.5 = bf16[8,8,8,512]{3,2,1,0:T(8,128)(2,1)} collective-permute-done((bf16[8,8,8,512]{3,2,1,0:T(8,128)(2,1)S(1)}, bf16[8,8,8,512]{3,2,1,0:T(8,128)(2,1)}, u32[]{:S(2)}, u32[]{:S(2)}) %collective-permute-start.5) | collective-permute-done | bytes 524320 | tf_op jit(solution)/shard_map/while/body/eval_jaxpr/ppermute | solution.py:29
  501.8 6.8 collective-permute-start.3
  513.6 6.8 conditional.5
  522.0 10.0 %collective-permute-done.5 = bf16[8,8,8,512]{3,2,1,0:T(8,128)(2,1)} collective-permute-done((bf16[8,8,8,512]{3,2,1,0:T(8,128)(2,1)S(1)}, bf16[8,8,8,512]{3,2,1,0:T(8,128)(2,1)}, u32[]{:S(2)}, u32[]{:S(2)}) %collective-permute-start.5) | collective-permute-done | bytes 524320 | tf_op jit(solution)/shard_map/while/body/eval_jaxpr/ppermute | solution.py:29
  535.5 6.8 collective-permute-start.3
  547.3 6.8 conditional.5
  555.7 8.5 %collective-permute-done.5 = bf16[8,8,8,512]{3,2,1,0:T(8,128)(2,1)} collective-permute-done((bf16[8,8,8,512]{3,2,1,0:T(8,128)(2,1)S(1)}, bf16[8,8,8,512]{3,2,1,0:T(8,128)(2,1)}, u32[]{:S(2)}, u32[]{:S(2)}) %collective-permute-start.5) | collective-permute-done | bytes 524320 | tf_op jit(solution)/shard_map/while/body/eval_jaxpr/ppermute | solution.py:29
  566.4 67.9 %all-reduce.4.cloned.1.call-done = bf16[16,8,8,512]{3,2,0,1:T(8,128)(2,1)} async-done(((bf16[16,8,8,512]{3,2,0,1:T(8,128)(2,1)}), bf16[16,8,8,512]{3,2,0,1:T(8,128)(2,1)}) %all-reduce.4.cloned.1.call-update) | async-done | bytes 1048592 | tf_op jit(solution)/shard_map/psum | solution.py:34
  636.0 79.2 %psum.22 = f32[16,16]{1,0:T(8,128)S(1)} all-reduce(f32[16,16]{1,0:T(8,128)S(1)} %convolution_multiply_fusion.1), channel_id=1, replica_groups=mesh['section'=8,'lon'=32] {'section','lon'}, use_global_device_ids=true, to_apply=%region_9.10 | all-reduce | flops 256 | bytes 2048 | tf_op jit(solution)/shard_map/psum | solution.py:159
  716.9 73.3 %psum.23 = f32[16,16]{1,0:T(8,128)} all-reduce(f32[16,16]{1,0:T(8,128)S(1)} %convolution_multiply_fusion), channel_id=1, replica_groups=mesh['section'=8,'lon'=32] {'section','lon'}, use_global_device_ids=true, to_apply=%region_10.11 | all-reduce | flops 256 | bytes 2048 | tf_op jit(solution)/shard_map/psum | solution.py:162
  (270 shorter events, 152.7 us)
Async XLA Ops:
  7.2 628.3 %copy-start = (f32[16,16]{1,0:T(8,128)S(1)}, f32[16,16]{1,0:T(8,128)}, u32[]{:S(2)}) copy-start(f32[16,16]{1,0:T(8,128)} %param.16) | copy-start | bytes 3076
  7.2 627.2 %all-reduce.4.cloned.1.call-start = ((), (), s32[]{:S(2)}) async-start(), calls=%async_computation | async-start | bytes 2097152 | tf_op jit(solution)/shard_map/psum | solution.py:34
  8.2 249.2 %copy-start.4 = (f32[8,8]{1,0:T(8,128)S(1)}, f32[8,8]{1,0:T(8,128)}, u32[]{:S(2)}) copy-start(f32[8,8]{1,0:T(8,128)} %param.19) | copy-start | bytes 772
  10.8 6.7 collective-permute-start
  14.0 4.0 collective-permute-start.1
  18.7 2.3 copy-start.1
  25.2 7.4 collective-permute-start.2
  35.1 11.0 %collective-permute-start = (bf16[8,8,4,512]{3,2,1,0:T(4,128)(2,1)S(1)}, bf16[8,8,4,512]{3,2,1,0:T(4,128)(2,1)S(1)}, u32[]{:S(2)}, u32[]{:S(2)}) collective-permute-start(bf16[8,8,4,512]{3,2,1,0:T(4,128)(2,1)S(1)} %get-tuple-element.424), channel_id=1, source_target_pairs={{1,0},{2,1},{3,2},{4,3},{5,4},{6,5},{7,6},{8,7},{9,8},{10,9},{11,1... | collective-permute-start | bytes 786440 | tf_op jit(solution)/shard_map/while/body/eval_jaxpr/ppermute | solution.py:19
  43.8 3.9 collective-permute-start.1
  48.4 2.3 copy-start.1
  54.9 9.9 %collective-permute-start.2 = (bf16[8,8,8,512]{3,2,1,0:T(8,128)(2,1)S(1)}, bf16[8,8,8,512]{3,2,1,0:T(8,128)(2,1)S(1)}, u32[]{:S(2)}, u32[]{:S(2)}) collective-permute-start(bf16[8,8,8,512]{3,2,1,0:T(8,128)(2,1)S(1)} %get-tuple-element.522), channel_id=1, source_target_pairs={{0,32},{32,64},{64,96},{96,128},{128,160},{160,192},{192,224},{1,3... | collective-permute-start | bytes 1572872 | tf_op jit(solution)/shard_map/while/body/eval_jaxpr/ppermute | solution.py:29
  67.3 10.2 %collective-permute-start = (bf16[8,8,4,512]{3,2,1,0:T(4,128)(2,1)S(1)}, bf16[8,8,4,512]{3,2,1,0:T(4,128)(2,1)S(1)}, u32[]{:S(2)}, u32[]{:S(2)}) collective-permute-start(bf16[8,8,4,512]{3,2,1,0:T(4,128)(2,1)S(1)} %get-tuple-element.424), channel_id=1, source_target_pairs={{1,0},{2,1},{3,2},{4,3},{5,4},{6,5},{7,6},{8,7},{9,8},{10,9},{11,1... | collective-permute-start | bytes 786440 | tf_op jit(solution)/shard_map/while/body/eval_jaxpr/ppermute | solution.py:19
  76.3 3.3 collective-permute-start.1
  80.4 16.7 %collective-permute-start.2 = (bf16[8,8,8,512]{3,2,1,0:T(8,128)(2,1)S(1)}, bf16[8,8,8,512]{3,2,1,0:T(8,128)(2,1)S(1)}, u32[]{:S(2)}, u32[]{:S(2)}) collective-permute-start(bf16[8,8,8,512]{3,2,1,0:T(8,128)(2,1)S(1)} %get-tuple-element.522), channel_id=1, source_target_pairs={{0,32},{32,64},{64,96},{96,128},{128,160},{160,192},{192,224},{1,3... | collective-permute-start | bytes 1572872 | tf_op jit(solution)/shard_map/while/body/eval_jaxpr/ppermute | solution.py:29
  99.6 9.3 %collective-permute-start = (bf16[8,8,4,512]{3,2,1,0:T(4,128)(2,1)S(1)}, bf16[8,8,4,512]{3,2,1,0:T(4,128)(2,1)S(1)}, u32[]{:S(2)}, u32[]{:S(2)}) collective-permute-start(bf16[8,8,4,512]{3,2,1,0:T(4,128)(2,1)S(1)} %get-tuple-element.424), channel_id=1, source_target_pairs={{1,0},{2,1},{3,2},{4,3},{5,4},{6,5},{7,6},{8,7},{9,8},{10,9},{11,1... | collective-permute-start | bytes 786440 | tf_op jit(solution)/shard_map/while/body/eval_jaxpr/ppermute | solution.py:19
  107.7 3.3 collective-permute-start.1
  111.7 10.2 %collective-permute-start.2 = (bf16[8,8,8,512]{3,2,1,0:T(8,128)(2,1)S(1)}, bf16[8,8,8,512]{3,2,1,0:T(8,128)(2,1)S(1)}, u32[]{:S(2)}, u32[]{:S(2)}) collective-permute-start(bf16[8,8,8,512]{3,2,1,0:T(8,128)(2,1)S(1)} %get-tuple-element.522), channel_id=1, source_target_pairs={{0,32},{32,64},{64,96},{96,128},{128,160},{160,192},{192,224},{1,3... | collective-permute-start | bytes 1572872 | tf_op jit(solution)/shard_map/while/body/eval_jaxpr/ppermute | solution.py:29
  124.4 8.3 %collective-permute-start = (bf16[8,8,4,512]{3,2,1,0:T(4,128)(2,1)S(1)}, bf16[8,8,4,512]{3,2,1,0:T(4,128)(2,1)S(1)}, u32[]{:S(2)}, u32[]{:S(2)}) collective-permute-start(bf16[8,8,4,512]{3,2,1,0:T(4,128)(2,1)S(1)} %get-tuple-element.424), channel_id=1, source_target_pairs={{1,0},{2,1},{3,2},{4,3},{5,4},{6,5},{7,6},{8,7},{9,8},{10,9},{11,1... | collective-permute-start | bytes 786440 | tf_op jit(solution)/shard_map/while/body/eval_jaxpr/ppermute | solution.py:19
  131.6 3.3 collective-permute-start.1
  135.7 14.8 %collective-permute-start.2 = (bf16[8,8,8,512]{3,2,1,0:T(8,128)(2,1)S(1)}, bf16[8,8,8,512]{3,2,1,0:T(8,128)(2,1)S(1)}, u32[]{:S(2)}, u32[]{:S(2)}) collective-permute-start(bf16[8,8,8,512]{3,2,1,0:T(8,128)(2,1)S(1)} %get-tuple-element.522), channel_id=1, source_target_pairs={{0,32},{32,64},{64,96},{96,128},{128,160},{160,192},{192,224},{1,3... | collective-permute-start | bytes 1572872 | tf_op jit(solution)/shard_map/while/body/eval_jaxpr/ppermute | solution.py:29
  152.9 8.6 %collective-permute-start = (bf16[8,8,4,512]{3,2,1,0:T(4,128)(2,1)S(1)}, bf16[8,8,4,512]{3,2,1,0:T(4,128)(2,1)S(1)}, u32[]{:S(2)}, u32[]{:S(2)}) collective-permute-start(bf16[8,8,4,512]{3,2,1,0:T(4,128)(2,1)S(1)} %get-tuple-element.424), channel_id=1, source_target_pairs={{1,0},{2,1},{3,2},{4,3},{5,4},{6,5},{7,6},{8,7},{9,8},{10,9},{11,1... | collective-permute-start | bytes 786440 | tf_op jit(solution)/shard_map/while/body/eval_jaxpr/ppermute | solution.py:19
  160.3 3.3 collective-permute-start.1
  164.4 10.2 %collective-permute-start.2 = (bf16[8,8,8,512]{3,2,1,0:T(8,128)(2,1)S(1)}, bf16[8,8,8,512]{3,2,1,0:T(8,128)(2,1)S(1)}, u32[]{:S(2)}, u32[]{:S(2)}) collective-permute-start(bf16[8,8,8,512]{3,2,1,0:T(8,128)(2,1)S(1)} %get-tuple-element.522), channel_id=1, source_target_pairs={{0,32},{32,64},{64,96},{96,128},{128,160},{160,192},{192,224},{1,3... | collective-permute-start | bytes 1572872 | tf_op jit(solution)/shard_map/while/body/eval_jaxpr/ppermute | solution.py:29
  177.1 8.0 %collective-permute-start = (bf16[8,8,4,512]{3,2,1,0:T(4,128)(2,1)S(1)}, bf16[8,8,4,512]{3,2,1,0:T(4,128)(2,1)S(1)}, u32[]{:S(2)}, u32[]{:S(2)}) collective-permute-start(bf16[8,8,4,512]{3,2,1,0:T(4,128)(2,1)S(1)} %get-tuple-element.424), channel_id=1, source_target_pairs={{1,0},{2,1},{3,2},{4,3},{5,4},{6,5},{7,6},{8,7},{9,8},{10,9},{11,1... | collective-permute-start | bytes 786440 | tf_op jit(solution)/shard_map/while/body/eval_jaxpr/ppermute | solution.py:19
  183.9 3.3 collective-permute-start.1
  188.0 14.8 %collective-permute-start.2 = (bf16[8,8,8,512]{3,2,1,0:T(8,128)(2,1)S(1)}, bf16[8,8,8,512]{3,2,1,0:T(8,128)(2,1)S(1)}, u32[]{:S(2)}, u32[]{:S(2)}) collective-permute-start(bf16[8,8,8,512]{3,2,1,0:T(8,128)(2,1)S(1)} %get-tuple-element.522), channel_id=1, source_target_pairs={{0,32},{32,64},{64,96},{96,128},{128,160},{160,192},{192,224},{1,3... | collective-permute-start | bytes 1572872 | tf_op jit(solution)/shard_map/while/body/eval_jaxpr/ppermute | solution.py:29
  205.2 8.0 %collective-permute-start = (bf16[8,8,4,512]{3,2,1,0:T(4,128)(2,1)S(1)}, bf16[8,8,4,512]{3,2,1,0:T(4,128)(2,1)S(1)}, u32[]{:S(2)}, u32[]{:S(2)}) collective-permute-start(bf16[8,8,4,512]{3,2,1,0:T(4,128)(2,1)S(1)} %get-tuple-element.424), channel_id=1, source_target_pairs={{1,0},{2,1},{3,2},{4,3},{5,4},{6,5},{7,6},{8,7},{9,8},{10,9},{11,1... | collective-permute-start | bytes 786440 | tf_op jit(solution)/shard_map/while/body/eval_jaxpr/ppermute | solution.py:19
  212.0 3.3 collective-permute-start.1
  216.1 10.2 %collective-permute-start.2 = (bf16[8,8,8,512]{3,2,1,0:T(8,128)(2,1)S(1)}, bf16[8,8,8,512]{3,2,1,0:T(8,128)(2,1)S(1)}, u32[]{:S(2)}, u32[]{:S(2)}) collective-permute-start(bf16[8,8,8,512]{3,2,1,0:T(8,128)(2,1)S(1)} %get-tuple-element.522), channel_id=1, source_target_pairs={{0,32},{32,64},{64,96},{96,128},{128,160},{160,192},{192,224},{1,3... | collective-permute-start | bytes 1572872 | tf_op jit(solution)/shard_map/while/body/eval_jaxpr/ppermute | solution.py:29
  228.8 8.0 %collective-permute-start = (bf16[8,8,4,512]{3,2,1,0:T(4,128)(2,1)S(1)}, bf16[8,8,4,512]{3,2,1,0:T(4,128)(2,1)S(1)}, u32[]{:S(2)}, u32[]{:S(2)}) collective-permute-start(bf16[8,8,4,512]{3,2,1,0:T(4,128)(2,1)S(1)} %get-tuple-element.424), channel_id=1, source_target_pairs={{1,0},{2,1},{3,2},{4,3},{5,4},{6,5},{7,6},{8,7},{9,8},{10,9},{11,1... | collective-permute-start | bytes 786440 | tf_op jit(solution)/shard_map/while/body/eval_jaxpr/ppermute | solution.py:19
  235.6 3.3 collective-permute-start.1
  239.7 16.8 %collective-permute-start.2 = (bf16[8,8,8,512]{3,2,1,0:T(8,128)(2,1)S(1)}, bf16[8,8,8,512]{3,2,1,0:T(8,128)(2,1)S(1)}, u32[]{:S(2)}, u32[]{:S(2)}) collective-permute-start(bf16[8,8,8,512]{3,2,1,0:T(8,128)(2,1)S(1)} %get-tuple-element.522), channel_id=1, source_target_pairs={{0,32},{32,64},{64,96},{96,128},{128,160},{160,192},{192,224},{1,3... | collective-permute-start | bytes 1572872 | tf_op jit(solution)/shard_map/while/body/eval_jaxpr/ppermute | solution.py:29
  261.0 8.2 %collective-permute-start.3 = (bf16[8,8,4,512]{3,2,1,0:T(4,128)(2,1)}, bf16[8,8,4,512]{3,2,1,0:T(4,128)(2,1)}, u32[]{:S(2)}, u32[]{:S(2)}) collective-permute-start(bf16[8,8,4,512]{3,2,1,0:T(4,128)(2,1)} %get-tuple-element.439), channel_id=1, source_target_pairs={{1,0},{2,1},{3,2},{4,3},{5,4},{6,5},{7,6},{8,7},{9,8},{10,9},{11,1... | collective-permute-start | bytes 786440 | tf_op jit(solution)/shard_map/while/body/eval_jaxpr/ppermute | solution.py:19
  267.8 3.3 collective-permute-start.4
  272.8 11.8 %collective-permute-start.5 = (bf16[8,8,8,512]{3,2,1,0:T(8,128)(2,1)S(1)}, bf16[8,8,8,512]{3,2,1,0:T(8,128)(2,1)}, u32[]{:S(2)}, u32[]{:S(2)}) collective-permute-start(bf16[8,8,8,512]{3,2,1,0:T(8,128)(2,1)S(1)} %get-tuple-element.523), channel_id=1, source_target_pairs={{32,0},{64,32},{96,64},{128,96},{160,128},{192,160},{224,192},{33,... | collective-permute-start | bytes 1572872 | tf_op jit(solution)/shard_map/while/body/eval_jaxpr/ppermute | solution.py:29
  288.2 8.3 %collective-permute-start.3 = (bf16[8,8,4,512]{3,2,1,0:T(4,128)(2,1)}, bf16[8,8,4,512]{3,2,1,0:T(4,128)(2,1)}, u32[]{:S(2)}, u32[]{:S(2)}) collective-permute-start(bf16[8,8,4,512]{3,2,1,0:T(4,128)(2,1)} %get-tuple-element.439), channel_id=1, source_target_pairs={{1,0},{2,1},{3,2},{4,3},{5,4},{6,5},{7,6},{8,7},{9,8},{10,9},{11,1... | collective-permute-start | bytes 786440 | tf_op jit(solution)/shard_map/while/body/eval_jaxpr/ppermute | solution.py:19
  295.0 3.3 collective-permute-start.4
  300.1 13.6 %collective-permute-start.5 = (bf16[8,8,8,512]{3,2,1,0:T(8,128)(2,1)S(1)}, bf16[8,8,8,512]{3,2,1,0:T(8,128)(2,1)}, u32[]{:S(2)}, u32[]{:S(2)}) collective-permute-start(bf16[8,8,8,512]{3,2,1,0:T(8,128)(2,1)S(1)} %get-tuple-element.523), channel_id=1, source_target_pairs={{32,0},{64,32},{96,64},{128,96},{160,128},{192,160},{224,192},{33,... | collective-permute-start | bytes 1572872 | tf_op jit(solution)/shard_map/while/body/eval_jaxpr/ppermute | solution.py:29
  317.2 8.3 %collective-permute-start.3 = (bf16[8,8,4,512]{3,2,1,0:T(4,128)(2,1)}, bf16[8,8,4,512]{3,2,1,0:T(4,128)(2,1)}, u32[]{:S(2)}, u32[]{:S(2)}) collective-permute-start(bf16[8,8,4,512]{3,2,1,0:T(4,128)(2,1)} %get-tuple-element.439), channel_id=1, source_target_pairs={{1,0},{2,1},{3,2},{4,3},{5,4},{6,5},{7,6},{8,7},{9,8},{10,9},{11,1... | collective-permute-start | bytes 786440 | tf_op jit(solution)/shard_map/while/body/eval_jaxpr/ppermute | solution.py:19
  323.9 3.3 collective-permute-start.4
  329.0 12.0 %collective-permute-start.5 = (bf16[8,8,8,512]{3,2,1,0:T(8,128)(2,1)S(1)}, bf16[8,8,8,512]{3,2,1,0:T(8,128)(2,1)}, u32[]{:S(2)}, u32[]{:S(2)}) collective-permute-start(bf16[8,8,8,512]{3,2,1,0:T(8,128)(2,1)S(1)} %get-tuple-element.523), channel_id=1, source_target_pairs={{32,0},{64,32},{96,64},{128,96},{160,128},{192,160},{224,192},{33,... | collective-permute-start | bytes 1572872 | tf_op jit(solution)/shard_map/while/body/eval_jaxpr/ppermute | solution.py:29
  344.6 8.3 %collective-permute-start.3 = (bf16[8,8,4,512]{3,2,1,0:T(4,128)(2,1)}, bf16[8,8,4,512]{3,2,1,0:T(4,128)(2,1)}, u32[]{:S(2)}, u32[]{:S(2)}) collective-permute-start(bf16[8,8,4,512]{3,2,1,0:T(4,128)(2,1)} %get-tuple-element.439), channel_id=1, source_target_pairs={{1,0},{2,1},{3,2},{4,3},{5,4},{6,5},{7,6},{8,7},{9,8},{10,9},{11,1... | collective-permute-start | bytes 786440 | tf_op jit(solution)/shard_map/while/body/eval_jaxpr/ppermute | solution.py:19
  351.4 3.3 collective-permute-start.4
  356.4 13.6 %collective-permute-start.5 = (bf16[8,8,8,512]{3,2,1,0:T(8,128)(2,1)S(1)}, bf16[8,8,8,512]{3,2,1,0:T(8,128)(2,1)}, u32[]{:S(2)}, u32[]{:S(2)}) collective-permute-start(bf16[8,8,8,512]{3,2,1,0:T(8,128)(2,1)S(1)} %get-tuple-element.523), channel_id=1, source_target_pairs={{32,0},{64,32},{96,64},{128,96},{160,128},{192,160},{224,192},{33,... | collective-permute-start | bytes 1572872 | tf_op jit(solution)/shard_map/while/body/eval_jaxpr/ppermute | solution.py:29
  373.6 8.3 %collective-permute-start.3 = (bf16[8,8,4,512]{3,2,1,0:T(4,128)(2,1)}, bf16[8,8,4,512]{3,2,1,0:T(4,128)(2,1)}, u32[]{:S(2)}, u32[]{:S(2)}) collective-permute-start(bf16[8,8,4,512]{3,2,1,0:T(4,128)(2,1)} %get-tuple-element.439), channel_id=1, source_target_pairs={{1,0},{2,1},{3,2},{4,3},{5,4},{6,5},{7,6},{8,7},{9,8},{10,9},{11,1... | collective-permute-start | bytes 786440 | tf_op jit(solution)/shard_map/while/body/eval_jaxpr/ppermute | solution.py:19
  380.3 3.3 collective-permute-start.4
  385.4 11.5 %collective-permute-start.5 = (bf16[8,8,8,512]{3,2,1,0:T(8,128)(2,1)S(1)}, bf16[8,8,8,512]{3,2,1,0:T(8,128)(2,1)}, u32[]{:S(2)}, u32[]{:S(2)}) collective-permute-start(bf16[8,8,8,512]{3,2,1,0:T(8,128)(2,1)S(1)} %get-tuple-element.523), channel_id=1, source_target_pairs={{32,0},{64,32},{96,64},{128,96},{160,128},{192,160},{224,192},{33,... | collective-permute-start | bytes 1572872 | tf_op jit(solution)/shard_map/while/body/eval_jaxpr/ppermute | solution.py:29
  400.5 8.3 %collective-permute-start.3 = (bf16[8,8,4,512]{3,2,1,0:T(4,128)(2,1)}, bf16[8,8,4,512]{3,2,1,0:T(4,128)(2,1)}, u32[]{:S(2)}, u32[]{:S(2)}) collective-permute-start(bf16[8,8,4,512]{3,2,1,0:T(4,128)(2,1)} %get-tuple-element.439), channel_id=1, source_target_pairs={{1,0},{2,1},{3,2},{4,3},{5,4},{6,5},{7,6},{8,7},{9,8},{10,9},{11,1... | collective-permute-start | bytes 786440 | tf_op jit(solution)/shard_map/while/body/eval_jaxpr/ppermute | solution.py:19
  407.3 3.3 collective-permute-start.4
  412.4 14.0 %collective-permute-start.5 = (bf16[8,8,8,512]{3,2,1,0:T(8,128)(2,1)S(1)}, bf16[8,8,8,512]{3,2,1,0:T(8,128)(2,1)}, u32[]{:S(2)}, u32[]{:S(2)}) collective-permute-start(bf16[8,8,8,512]{3,2,1,0:T(8,128)(2,1)S(1)} %get-tuple-element.523), channel_id=1, source_target_pairs={{32,0},{64,32},{96,64},{128,96},{160,128},{192,160},{224,192},{33,... | collective-permute-start | bytes 1572872 | tf_op jit(solution)/shard_map/while/body/eval_jaxpr/ppermute | solution.py:29
  429.9 8.3 %collective-permute-start.3 = (bf16[8,8,4,512]{3,2,1,0:T(4,128)(2,1)}, bf16[8,8,4,512]{3,2,1,0:T(4,128)(2,1)}, u32[]{:S(2)}, u32[]{:S(2)}) collective-permute-start(bf16[8,8,4,512]{3,2,1,0:T(4,128)(2,1)} %get-tuple-element.439), channel_id=1, source_target_pairs={{1,0},{2,1},{3,2},{4,3},{5,4},{6,5},{7,6},{8,7},{9,8},{10,9},{11,1... | collective-permute-start | bytes 786440 | tf_op jit(solution)/shard_map/while/body/eval_jaxpr/ppermute | solution.py:19
  436.7 3.3 collective-permute-start.4
  441.8 56.5 %collective-permute-start.5 = (bf16[8,8,8,512]{3,2,1,0:T(8,128)(2,1)S(1)}, bf16[8,8,8,512]{3,2,1,0:T(8,128)(2,1)}, u32[]{:S(2)}, u32[]{:S(2)}) collective-permute-start(bf16[8,8,8,512]{3,2,1,0:T(8,128)(2,1)S(1)} %get-tuple-element.523), channel_id=1, source_target_pairs={{32,0},{64,32},{96,64},{128,96},{160,128},{192,160},{224,192},{33,... | collective-permute-start | bytes 1572872 | tf_op jit(solution)/shard_map/while/body/eval_jaxpr/ppermute | solution.py:29
  501.8 8.3 %collective-permute-start.3 = (bf16[8,8,4,512]{3,2,1,0:T(4,128)(2,1)}, bf16[8,8,4,512]{3,2,1,0:T(4,128)(2,1)}, u32[]{:S(2)}, u32[]{:S(2)}) collective-permute-start(bf16[8,8,4,512]{3,2,1,0:T(4,128)(2,1)} %get-tuple-element.439), channel_id=1, source_target_pairs={{1,0},{2,1},{3,2},{4,3},{5,4},{6,5},{7,6},{8,7},{9,8},{10,9},{11,1... | collective-permute-start | bytes 786440 | tf_op jit(solution)/shard_map/while/body/eval_jaxpr/ppermute | solution.py:19
  508.6 3.3 collective-permute-start.4
  513.6 2.3 copy-start.2
  520.4 11.5 %collective-permute-start.5 = (bf16[8,8,8,512]{3,2,1,0:T(8,128)(2,1)S(1)}, bf16[8,8,8,512]{3,2,1,0:T(8,128)(2,1)}, u32[]{:S(2)}, u32[]{:S(2)}) collective-permute-start(bf16[8,8,8,512]{3,2,1,0:T(8,128)(2,1)S(1)} %get-tuple-element.523), channel_id=1, source_target_pairs={{32,0},{64,32},{96,64},{128,96},{160,128},{192,160},{224,192},{33,... | collective-permute-start | bytes 1572872 | tf_op jit(solution)/shard_map/while/body/eval_jaxpr/ppermute | solution.py:29
  535.5 8.3 %collective-permute-start.3 = (bf16[8,8,4,512]{3,2,1,0:T(4,128)(2,1)}, bf16[8,8,4,512]{3,2,1,0:T(4,128)(2,1)}, u32[]{:S(2)}, u32[]{:S(2)}) collective-permute-start(bf16[8,8,4,512]{3,2,1,0:T(4,128)(2,1)} %get-tuple-element.439), channel_id=1, source_target_pairs={{1,0},{2,1},{3,2},{4,3},{5,4},{6,5},{7,6},{8,7},{9,8},{10,9},{11,1... | collective-permute-start | bytes 786440 | tf_op jit(solution)/shard_map/while/body/eval_jaxpr/ppermute | solution.py:19
  542.3 3.3 collective-permute-start.4
  547.3 2.3 copy-start.2
  554.2 10.0 %collective-permute-start.5 = (bf16[8,8,8,512]{3,2,1,0:T(8,128)(2,1)S(1)}, bf16[8,8,8,512]{3,2,1,0:T(8,128)(2,1)}, u32[]{:S(2)}, u32[]{:S(2)}) collective-permute-start(bf16[8,8,8,512]{3,2,1,0:T(8,128)(2,1)S(1)} %get-tuple-element.523), channel_id=1, source_target_pairs={{32,0},{64,32},{96,64},{128,96},{160,128},{192,160},{224,192},{33,... | collective-permute-start | bytes 1572872 | tf_op jit(solution)/shard_map/while/body/eval_jaxpr/ppermute | solution.py:29
  564.2 1.2 copy-start.3
  715.2 75.0 %copy-start.5 = (f32[16,16]{1,0:T(8,128)}, f32[16,16]{1,0:T(8,128)S(1)}, u32[]{:S(2)}) copy-start(f32[16,16]{1,0:T(8,128)S(1)} %psum.22) | copy-start | bytes 3076
Sparse Core Ops, SparseCore 0:
  565.5 68.8 all-reduce.3
where the time goes:
time: 799 us; the launch traced here: 797 us
  waiting for transfers between devices  322 us (40%)
  starting transfers between devices  193 us (24%)
  blocking collectives  153 us (19%)
  other arithmetic  49.3 us (6%)
  local copies, waits for them, and re-layouts  35.4 us (4%)
  matrix products  17.6 us (2%)
  between operations  14.2 us (2%)
  loops' own time  12.5 us (2%)
    ppermute x18, waiting for transfers between devices, from_behind(): return lax.ppermute(shard, axis, pairs)  193 us
    ppermute x18, starting transfers between devices, padded(): lax.ppermute(head, axis, [((i + 1) % count, i) for i in range(count)])  125 us
    psum x1, blocking collectives, body(): projection = lax.psum(part_projection, ('section', 'lon'))  79.2 us
    psum x1, blocking collectives, body(): residual_gram = lax.psum(part_gram, ('section', 'lon'))  73.3 us
    psum x1, waiting for transfers between devices, broadcast(): return lax.psum(jnp.where(mine, shard, jnp.zeros_like(shard)), axis)  67.9 us
    ppermute x18, starting transfers between devices, from_behind(): return lax.ppermute(shard, axis, pairs)  67.9 us
    ppermute x18, waiting for transfers between devices, padded(): lax.ppermute(tail, axis, [(i, (i + 1) % count) for i in range(count)])  33.5 us
    ppermute x18, waiting for transfers between devices, padded(): lax.ppermute(head, axis, [((i + 1) % count, i) for i in range(count)])  27.4 us
  transfers between devices with their start and end apart: 55, of which 55 were waited for; matrix products, arithmetic and copies ran while one was open for 1% of the time, Pallas kernels for 0%

commit v1 on v0

--- a/solution.py
+++ b/solution.py
@@ -156,7 +156,7 @@
         beta_prev, prev_flat, precision=high
     )
     part_projection = jnp.dot(block_flat, shifted.T, precision=high) / cell_count
-    projection = lax.psum(part_projection, ("section", "lon"))
+    projection = lax.psum(lax.psum(part_projection, "lon"), "section")
     residual_rows = shifted - jnp.dot(projection.T, block_flat, precision=high)
     part_gram = jnp.dot(residual_rows, residual_rows.T, precision=high) / cell_count
     residual_gram = lax.psum(part_gram, ("section", "lon"))

time: 799 us -> 804 us (level)
    psum x1 -> x2, blocking collectives: 79.2 us -> 81.2 us  [body(): projection = lax.psum(lax.psum(part_projection, 'lon'), 'section')]
where the time goes in v1:
time: 804 us; the launch traced here: 802 us
  waiting for transfers between devices  322 us (40%)
  starting transfers between devices  193 us (24%)
  blocking collectives  156 us (19%)
  other arithmetic  49.3 us (6%)
  local copies, waits for them, and re-layouts  36 us (4%)
  matrix products  17.6 us (2%)
  between operations  14.2 us (2%)
  loops' own time  13.3 us (2%)
    ppermute x18, waiting for transfers between devices, from_behind(): return lax.ppermute(shard, axis, pairs)  193 us
    ppermute x18, starting transfers between devices, padded(): lax.ppermute(head, axis, [((i + 1) % count, i) for i in range(count)])  125 us
    psum x2, blocking collectives, body(): projection = lax.psum(lax.psum(part_projection, 'lon'), 'section')  81.2 us
    psum x1, blocking collectives, body(): residual_gram = lax.psum(part_gram, ('section', 'lon'))  74.7 us
    ppermute x18, starting transfers between devices, from_behind(): return lax.ppermute(shard, axis, pairs)  67.9 us
    psum x1, waiting for transfers between devices, broadcast(): return lax.psum(jnp.where(mine, shard, jnp.zeros_like(shard)), axis)  67.9 us
    ppermute x18, waiting for transfers between devices, padded(): lax.ppermute(tail, axis, [(i, (i + 1) % count) for i in range(count)])  33.5 us
    ppermute x18, waiting for transfers between devices, padded(): lax.ppermute(head, axis, [((i + 1) % count, i) for i in range(count)])  27.4 us
  transfers between devices with their start and end apart: 55, of which 55 were waited for; matrix products, arithmetic and copies ran while one was open for 1% of the time, Pallas kernels for 0%

profile of v1, /device:TPU:1, one launch (start us, length us, event | category | flops | bytes accessed | tf_op | source)
XLA Modules:
  0.0 801.7 jit_solution(9775872552224720644)
XLA Ops:
  8.3 249.6 %while.27 = (s32[]{:T(128)}, bf16[8,8,8,512]{3,2,1,0:T(8,128)(2,1)S(1)}, bf16[2,8,8,8,512]{4,3,2,1,0:T(8,128)(2,1)S(1)}, s32[9]{0:T(128)S(1)}, s32[]{:T(128)}, /...) while((s32[]{:T(128)}, ...), condition=%wide.region_3.4_spmd, body=%wide.region_0.3_spmd.sunk | while | flops 2422734848 | bytes 67240344 | solution.py:106
  10.9 3.3 collective-permute-start
  14.2 3.4 collective-permute-done
  18.8 6.5 conditional.4
  26.9 5.8 collective-permute-done.2
  35.4 8.7 %collective-permute-start = (bf16[8,8,4,512]{3,2,1,0:T(4,128)(2,1)S(1)}, bf16[8,8,4,512]{3,2,1,0:T(4,128)(2,1)S(1)}, u32[]{:S(2)}, u32[]{:S(2)}) collective-permute-start(bf16[8,8,4,512]{3,2,1,0:T(4,128)(2,1)S(1)} %get-tuple-element.424), channel_id=1, source_target_pairs={{1,0},{2,1},{3,2},{4,3},{5,4},{6,5},{7,6},{8,7},{9,8},{10,9},{11,1... | collective-permute-start | bytes 786440 | tf_op jit(solution)/shard_map/while/body/eval_jaxpr/ppermute | solution.py:19
  44.1 2.3 collective-permute-done
  48.7 6.5 conditional.4
  55.2 3.8 collective-permute-start.2
  59.3 5.8 collective-permute-done.2
  67.8 9.0 %collective-permute-start = (bf16[8,8,4,512]{3,2,1,0:T(4,128)(2,1)S(1)}, bf16[8,8,4,512]{3,2,1,0:T(4,128)(2,1)S(1)}, u32[]{:S(2)}, u32[]{:S(2)}) collective-permute-start(bf16[8,8,4,512]{3,2,1,0:T(4,128)(2,1)S(1)} %get-tuple-element.424), channel_id=1, source_target_pairs={{1,0},{2,1},{3,2},{4,3},{5,4},{6,5},{7,6},{8,7},{9,8},{10,9},{11,1... | collective-permute-start | bytes 786440 | tf_op jit(solution)/shard_map/while/body/eval_jaxpr/ppermute | solution.py:19
  78.0 2.1 collective-permute-done.1
  80.9 10.6 %collective-permute-start.2 = (bf16[8,8,8,512]{3,2,1,0:T(8,128)(2,1)S(1)}, bf16[8,8,8,512]{3,2,1,0:T(8,128)(2,1)S(1)}, u32[]{:S(2)}, u32[]{:S(2)}) collective-permute-start(bf16[8,8,8,512]{3,2,1,0:T(8,128)(2,1)S(1)} %get-tuple-element.522), channel_id=1, source_target_pairs={{0,32},{32,64},{64,96},{96,128},{128,160},{160,192},{192,224},{1,3... | collective-permute-start | bytes 1572872 | tf_op jit(solution)/shard_map/while/body/eval_jaxpr/ppermute | solution.py:29
  91.7 5.8 collective-permute-done.2
  100.2 8.1 %collective-permute-start = (bf16[8,8,4,512]{3,2,1,0:T(4,128)(2,1)S(1)}, bf16[8,8,4,512]{3,2,1,0:T(4,128)(2,1)S(1)}, u32[]{:S(2)}, u32[]{:S(2)}) collective-permute-start(bf16[8,8,4,512]{3,2,1,0:T(4,128)(2,1)S(1)} %get-tuple-element.424), channel_id=1, source_target_pairs={{1,0},{2,1},{3,2},{4,3},{5,4},{6,5},{7,6},{8,7},{9,8},{10,9},{11,1... | collective-permute-start | bytes 786440 | tf_op jit(solution)/shard_map/while/body/eval_jaxpr/ppermute | solution.py:19
  109.4 2.2 collective-permute-done.1
  112.3 4.1 collective-permute-start.2
  116.7 5.8 collective-permute-done.2
  125.2 7.2 collective-permute-start
  133.5 2.2 collective-permute-done.1
  136.4 8.7 %collective-permute-start.2 = (bf16[8,8,8,512]{3,2,1,0:T(8,128)(2,1)S(1)}, bf16[8,8,8,512]{3,2,1,0:T(8,128)(2,1)S(1)}, u32[]{:S(2)}, u32[]{:S(2)}) collective-permute-start(bf16[8,8,8,512]{3,2,1,0:T(8,128)(2,1)S(1)} %get-tuple-element.522), channel_id=1, source_target_pairs={{0,32},{32,64},{64,96},{96,128},{128,160},{160,192},{192,224},{1,3... | collective-permute-start | bytes 1572872 | tf_op jit(solution)/shard_map/while/body/eval_jaxpr/ppermute | solution.py:29
  145.3 5.8 collective-permute-done.2
  153.8 7.4 collective-permute-start
  162.4 2.2 collective-permute-done.1
  165.3 4.1 collective-permute-start.2
  169.7 5.8 collective-permute-done.2
  178.1 6.8 collective-permute-start
  186.1 2.2 collective-permute-done.1
  189.0 8.7 %collective-permute-start.2 = (bf16[8,8,8,512]{3,2,1,0:T(8,128)(2,1)S(1)}, bf16[8,8,8,512]{3,2,1,0:T(8,128)(2,1)S(1)}, u32[]{:S(2)}, u32[]{:S(2)}) collective-permute-start(bf16[8,8,8,512]{3,2,1,0:T(8,128)(2,1)S(1)} %get-tuple-element.522), channel_id=1, source_target_pairs={{0,32},{32,64},{64,96},{96,128},{128,160},{160,192},{192,224},{1,3... | collective-permute-start | bytes 1572872 | tf_op jit(solution)/shard_map/while/body/eval_jaxpr/ppermute | solution.py:29
  197.9 5.8 collective-permute-done.2
  206.4 6.8 collective-permute-start
  214.4 2.2 collective-permute-done.1
  217.3 4.1 collective-permute-start.2
  221.7 5.8 collective-permute-done.2
  230.1 6.8 collective-permute-start
  238.1 2.2 collective-permute-done.1
  241.0 10.7 %collective-permute-start.2 = (bf16[8,8,8,512]{3,2,1,0:T(8,128)(2,1)S(1)}, bf16[8,8,8,512]{3,2,1,0:T(8,128)(2,1)S(1)}, u32[]{:S(2)}, u32[]{:S(2)}) collective-permute-start(bf16[8,8,8,512]{3,2,1,0:T(8,128)(2,1)S(1)} %get-tuple-element.522), channel_id=1, source_target_pairs={{0,32},{32,64},{64,96},{96,128},{128,160},{160,192},{192,224},{1,3... | collective-permute-start | bytes 1572872 | tf_op jit(solution)/shard_map/while/body/eval_jaxpr/ppermute | solution.py:29
  252.0 5.8 collective-permute-done.2
  258.8 306.7 %while.28 = (s32[]{:T(128)}, bf16[8,8,8,512]{3,2,1,0:T(8,128)(2,1)}, bf16[2,8,8,8,512]{4,3,2,1,0:T(8,128)(2,1)S(1)}, s32[9]{0:T(128)S(1)}, s32[]{:T(128)}, /*ind...) while((s32[]{:T(128)}, ...), condition=%wide.region_7.8_spmd, body=%wide.region_4.7_spmd.sunk | while | flops 2424045568 | bytes 67764888 | solution.py:138
  262.3 6.7 collective-permute-start.3
  275.7 10.3 %collective-permute-done.5 = bf16[8,8,8,512]{3,2,1,0:T(8,128)(2,1)} collective-permute-done((bf16[8,8,8,512]{3,2,1,0:T(8,128)(2,1)S(1)}, bf16[8,8,8,512]{3,2,1,0:T(8,128)(2,1)}, u32[]{:S(2)}, u32[]{:S(2)}) %collective-permute-start.5) | collective-permute-done | bytes 524320 | tf_op jit(solution)/shard_map/while/body/eval_jaxpr/ppermute | solution.py:29
  289.5 6.8 collective-permute-start.3
  302.9 12.0 %collective-permute-done.5 = bf16[8,8,8,512]{3,2,1,0:T(8,128)(2,1)} collective-permute-done((bf16[8,8,8,512]{3,2,1,0:T(8,128)(2,1)S(1)}, bf16[8,8,8,512]{3,2,1,0:T(8,128)(2,1)}, u32[]{:S(2)}, u32[]{:S(2)}) %collective-permute-start.5) | collective-permute-done | bytes 524320 | tf_op jit(solution)/shard_map/while/body/eval_jaxpr/ppermute | solution.py:29
  318.5 6.8 collective-permute-start.3
  331.9 10.5 %collective-permute-done.5 = bf16[8,8,8,512]{3,2,1,0:T(8,128)(2,1)} collective-permute-done((bf16[8,8,8,512]{3,2,1,0:T(8,128)(2,1)S(1)}, bf16[8,8,8,512]{3,2,1,0:T(8,128)(2,1)}, u32[]{:S(2)}, u32[]{:S(2)}) %collective-permute-start.5) | collective-permute-done | bytes 524320 | tf_op jit(solution)/shard_map/while/body/eval_jaxpr/ppermute | solution.py:29
  345.9 6.8 collective-permute-start.3
  354.2 1.8 collective-permute-done.4
  359.3 12.0 %collective-permute-done.5 = bf16[8,8,8,512]{3,2,1,0:T(8,128)(2,1)} collective-permute-done((bf16[8,8,8,512]{3,2,1,0:T(8,128)(2,1)S(1)}, bf16[8,8,8,512]{3,2,1,0:T(8,128)(2,1)}, u32[]{:S(2)}, u32[]{:S(2)}) %collective-permute-start.5) | collective-permute-done | bytes 524320 | tf_op jit(solution)/shard_map/while/body/eval_jaxpr/ppermute | solution.py:29
  374.9 6.8 collective-permute-start.3
  388.3 10.0 %collective-permute-done.5 = bf16[8,8,8,512]{3,2,1,0:T(8,128)(2,1)} collective-permute-done((bf16[8,8,8,512]{3,2,1,0:T(8,128)(2,1)S(1)}, bf16[8,8,8,512]{3,2,1,0:T(8,128)(2,1)}, u32[]{:S(2)}, u32[]{:S(2)}) %collective-permute-start.5) | collective-permute-done | bytes 524320 | tf_op jit(solution)/shard_map/while/body/eval_jaxpr/ppermute | solution.py:29
  401.8 6.8 collective-permute-start.3
  415.2 12.5 %collective-permute-done.5 = bf16[8,8,8,512]{3,2,1,0:T(8,128)(2,1)} collective-permute-done((bf16[8,8,8,512]{3,2,1,0:T(8,128)(2,1)S(1)}, bf16[8,8,8,512]{3,2,1,0:T(8,128)(2,1)}, u32[]{:S(2)}, u32[]{:S(2)}) %collective-permute-start.5) | collective-permute-done | bytes 524320 | tf_op jit(solution)/shard_map/while/body/eval_jaxpr/ppermute | solution.py:29
  431.3 6.8 collective-permute-start.3
  444.6 54.9 %collective-permute-done.5 = bf16[8,8,8,512]{3,2,1,0:T(8,128)(2,1)} collective-permute-done((bf16[8,8,8,512]{3,2,1,0:T(8,128)(2,1)S(1)}, bf16[8,8,8,512]{3,2,1,0:T(8,128)(2,1)}, u32[]{:S(2)}, u32[]{:S(2)}) %collective-permute-start.5) | collective-permute-done | bytes 524320 | tf_op jit(solution)/shard_map/while/body/eval_jaxpr/ppermute | solution.py:29
  503.1 6.8 collective-permute-start.3
  514.9 6.8 conditional.5
  523.3 10.0 %collective-permute-done.5 = bf16[8,8,8,512]{3,2,1,0:T(8,128)(2,1)} collective-permute-done((bf16[8,8,8,512]{3,2,1,0:T(8,128)(2,1)S(1)}, bf16[8,8,8,512]{3,2,1,0:T(8,128)(2,1)}, u32[]{:S(2)}, u32[]{:S(2)}) %collective-permute-start.5) | collective-permute-done | bytes 524320 | tf_op jit(solution)/shard_map/while/body/eval_jaxpr/ppermute | solution.py:29
  536.8 6.8 collective-permute-start.3
  548.6 6.8 conditional.5
  557.0 8.5 %collective-permute-done.5 = bf16[8,8,8,512]{3,2,1,0:T(8,128)(2,1)} collective-permute-done((bf16[8,8,8,512]{3,2,1,0:T(8,128)(2,1)S(1)}, bf16[8,8,8,512]{3,2,1,0:T(8,128)(2,1)}, u32[]{:S(2)}, u32[]{:S(2)}) %collective-permute-start.5) | collective-permute-done | bytes 524320 | tf_op jit(solution)/shard_map/while/body/eval_jaxpr/ppermute | solution.py:29
  567.7 67.9 %all-reduce.4.cloned.1.call-done = bf16[16,8,8,512]{3,2,0,1:T(8,128)(2,1)} async-done(((bf16[16,8,8,512]{3,2,0,1:T(8,128)(2,1)}), bf16[16,8,8,512]{3,2,0,1:T(8,128)(2,1)}) %all-reduce.4.cloned.1.call-update) | async-done | bytes 1048592 | tf_op jit(solution)/shard_map/psum | solution.py:34
  637.3 68.1 %psum.29 = f32[16,16]{1,0:T(8,128)S(1)} all-reduce(f32[16,16]{1,0:T(8,128)S(1)} %convolution_multiply_fusion.1), channel_id=1, replica_groups=mesh['section'=8,'lon'=32] {'lon'}, use_global_device_ids=true, to_apply=%region_9.10 | all-reduce | flops 256 | bytes 2048 | tf_op jit(solution)/shard_map/psum | solution.py:159
  705.4 13.1 %psum.30 = f32[16,16]{1,0:T(8,128)S(1)} all-reduce(f32[16,16]{1,0:T(8,128)S(1)} %psum.29), channel_id=1, replica_groups=mesh['section'=8,'lon'=32] {'section'}, use_global_device_ids=true, to_apply=%region_10.11 | all-reduce | flops 256 | bytes 2048 | tf_op jit(solution)/shard_map/psum | solution.py:159
  720.1 74.7 %psum.31 = f32[16,16]{1,0:T(8,128)} all-reduce(f32[16,16]{1,0:T(8,128)S(1)} %convolution_multiply_fusion), channel_id=1, replica_groups=mesh['section'=8,'lon'=32] {'section','lon'}, use_global_device_ids=true, to_apply=%region_11.12 | all-reduce | flops 256 | bytes 2048 | tf_op jit(solution)/shard_map/psum | solution.py:162
  (271 shorter events, 155.1 us)
Async XLA Ops:
  7.2 629.6 %copy-start = (f32[16,16]{1,0:T(8,128)S(1)}, f32[16,16]{1,0:T(8,128)}, u32[]{:S(2)}) copy-start(f32[16,16]{1,0:T(8,128)} %param.16) | copy-start | bytes 3076
  7.2 628.4 %all-reduce.4.cloned.1.call-start = ((), (), s32[]{:S(2)}) async-start(), calls=%async_computation | async-start | bytes 2097152 | tf_op jit(solution)/shard_map/psum | solution.py:34
  8.2 250.5 %copy-start.4 = (f32[8,8]{1,0:T(8,128)S(1)}, f32[8,8]{1,0:T(8,128)}, u32[]{:S(2)}) copy-start(f32[8,8]{1,0:T(8,128)} %param.19) | copy-start | bytes 772
  10.9 6.7 collective-permute-start
  14.2 4.0 collective-permute-start.1
  18.8 2.3 copy-start.1
  25.4 7.4 collective-permute-start.2
  35.4 11.0 %collective-permute-start = (bf16[8,8,4,512]{3,2,1,0:T(4,128)(2,1)S(1)}, bf16[8,8,4,512]{3,2,1,0:T(4,128)(2,1)S(1)}, u32[]{:S(2)}, u32[]{:S(2)}) collective-permute-start(bf16[8,8,4,512]{3,2,1,0:T(4,128)(2,1)S(1)} %get-tuple-element.424), channel_id=1, source_target_pairs={{1,0},{2,1},{3,2},{4,3},{5,4},{6,5},{7,6},{8,7},{9,8},{10,9},{11,1... | collective-permute-start | bytes 786440 | tf_op jit(solution)/shard_map/while/body/eval_jaxpr/ppermute | solution.py:19
  44.1 3.9 collective-permute-start.1
  48.7 2.3 copy-start.1
  55.2 9.9 %collective-permute-start.2 = (bf16[8,8,8,512]{3,2,1,0:T(8,128)(2,1)S(1)}, bf16[8,8,8,512]{3,2,1,0:T(8,128)(2,1)S(1)}, u32[]{:S(2)}, u32[]{:S(2)}) collective-permute-start(bf16[8,8,8,512]{3,2,1,0:T(8,128)(2,1)S(1)} %get-tuple-element.522), channel_id=1, source_target_pairs={{0,32},{32,64},{64,96},{96,128},{128,160},{160,192},{192,224},{1,3... | collective-permute-start | bytes 1572872 | tf_op jit(solution)/shard_map/while/body/eval_jaxpr/ppermute | solution.py:29
  67.8 10.2 %collective-permute-start = (bf16[8,8,4,512]{3,2,1,0:T(4,128)(2,1)S(1)}, bf16[8,8,4,512]{3,2,1,0:T(4,128)(2,1)S(1)}, u32[]{:S(2)}, u32[]{:S(2)}) collective-permute-start(bf16[8,8,4,512]{3,2,1,0:T(4,128)(2,1)S(1)} %get-tuple-element.424), channel_id=1, source_target_pairs={{1,0},{2,1},{3,2},{4,3},{5,4},{6,5},{7,6},{8,7},{9,8},{10,9},{11,1... | collective-permute-start | bytes 786440 | tf_op jit(solution)/shard_map/while/body/eval_jaxpr/ppermute | solution.py:19
  76.8 3.3 collective-permute-start.1
  80.9 16.7 %collective-permute-start.2 = (bf16[8,8,8,512]{3,2,1,0:T(8,128)(2,1)S(1)}, bf16[8,8,8,512]{3,2,1,0:T(8,128)(2,1)S(1)}, u32[]{:S(2)}, u32[]{:S(2)}) collective-permute-start(bf16[8,8,8,512]{3,2,1,0:T(8,128)(2,1)S(1)} %get-tuple-element.522), channel_id=1, source_target_pairs={{0,32},{32,64},{64,96},{96,128},{128,160},{160,192},{192,224},{1,3... | collective-permute-start | bytes 1572872 | tf_op jit(solution)/shard_map/while/body/eval_jaxpr/ppermute | solution.py:29
  100.2 9.3 %collective-permute-start = (bf16[8,8,4,512]{3,2,1,0:T(4,128)(2,1)S(1)}, bf16[8,8,4,512]{3,2,1,0:T(4,128)(2,1)S(1)}, u32[]{:S(2)}, u32[]{:S(2)}) collective-permute-start(bf16[8,8,4,512]{3,2,1,0:T(4,128)(2,1)S(1)} %get-tuple-element.424), channel_id=1, source_target_pairs={{1,0},{2,1},{3,2},{4,3},{5,4},{6,5},{7,6},{8,7},{9,8},{10,9},{11,1... | collective-permute-start | bytes 786440 | tf_op jit(solution)/shard_map/while/body/eval_jaxpr/ppermute | solution.py:19
  108.3 3.3 collective-permute-start.1
  112.3 10.2 %collective-permute-start.2 = (bf16[8,8,8,512]{3,2,1,0:T(8,128)(2,1)S(1)}, bf16[8,8,8,512]{3,2,1,0:T(8,128)(2,1)S(1)}, u32[]{:S(2)}, u32[]{:S(2)}) collective-permute-start(bf16[8,8,8,512]{3,2,1,0:T(8,128)(2,1)S(1)} %get-tuple-element.522), channel_id=1, source_target_pairs={{0,32},{32,64},{64,96},{96,128},{128,160},{160,192},{192,224},{1,3... | collective-permute-start | bytes 1572872 | tf_op jit(solution)/shard_map/while/body/eval_jaxpr/ppermute | solution.py:29
  125.2 8.3 %collective-permute-start = (bf16[8,8,4,512]{3,2,1,0:T(4,128)(2,1)S(1)}, bf16[8,8,4,512]{3,2,1,0:T(4,128)(2,1)S(1)}, u32[]{:S(2)}, u32[]{:S(2)}) collective-permute-start(bf16[8,8,4,512]{3,2,1,0:T(4,128)(2,1)S(1)} %get-tuple-element.424), channel_id=1, source_target_pairs={{1,0},{2,1},{3,2},{4,3},{5,4},{6,5},{7,6},{8,7},{9,8},{10,9},{11,1... | collective-permute-start | bytes 786440 | tf_op jit(solution)/shard_map/while/body/eval_jaxpr/ppermute | solution.py:19
  132.3 3.3 collective-permute-start.1
  136.4 14.8 %collective-permute-start.2 = (bf16[8,8,8,512]{3,2,1,0:T(8,128)(2,1)S(1)}, bf16[8,8,8,512]{3,2,1,0:T(8,128)(2,1)S(1)}, u32[]{:S(2)}, u32[]{:S(2)}) collective-permute-start(bf16[8,8,8,512]{3,2,1,0:T(8,128)(2,1)S(1)} %get-tuple-element.522), channel_id=1, source_target_pairs={{0,32},{32,64},{64,96},{96,128},{128,160},{160,192},{192,224},{1,3... | collective-permute-start | bytes 1572872 | tf_op jit(solution)/shard_map/while/body/eval_jaxpr/ppermute | solution.py:29
  153.8 8.6 %collective-permute-start = (bf16[8,8,4,512]{3,2,1,0:T(4,128)(2,1)S(1)}, bf16[8,8,4,512]{3,2,1,0:T(4,128)(2,1)S(1)}, u32[]{:S(2)}, u32[]{:S(2)}) collective-permute-start(bf16[8,8,4,512]{3,2,1,0:T(4,128)(2,1)S(1)} %get-tuple-element.424), channel_id=1, source_target_pairs={{1,0},{2,1},{3,2},{4,3},{5,4},{6,5},{7,6},{8,7},{9,8},{10,9},{11,1... | collective-permute-start | bytes 786440 | tf_op jit(solution)/shard_map/while/body/eval_jaxpr/ppermute | solution.py:19
  161.2 3.3 collective-permute-start.1
  165.3 10.2 %collective-permute-start.2 = (bf16[8,8,8,512]{3,2,1,0:T(8,128)(2,1)S(1)}, bf16[8,8,8,512]{3,2,1,0:T(8,128)(2,1)S(1)}, u32[]{:S(2)}, u32[]{:S(2)}) collective-permute-start(bf16[8,8,8,512]{3,2,1,0:T(8,128)(2,1)S(1)} %get-tuple-element.522), channel_id=1, source_target_pairs={{0,32},{32,64},{64,96},{96,128},{128,160},{160,192},{192,224},{1,3... | collective-permute-start | bytes 1572872 | tf_op jit(solution)/shard_map/while/body/eval_jaxpr/ppermute | solution.py:29
  178.1 8.0 collective-permute-start
  184.9 3.3 collective-permute-start.1
  189.0 14.8 %collective-permute-start.2 = (bf16[8,8,8,512]{3,2,1,0:T(8,128)(2,1)S(1)}, bf16[8,8,8,512]{3,2,1,0:T(8,128)(2,1)S(1)}, u32[]{:S(2)}, u32[]{:S(2)}) collective-permute-start(bf16[8,8,8,512]{3,2,1,0:T(8,128)(2,1)S(1)} %get-tuple-element.522), channel_id=1, source_target_pairs={{0,32},{32,64},{64,96},{96,128},{128,160},{160,192},{192,224},{1,3... | collective-permute-start | bytes 1572872 | tf_op jit(solution)/shard_map/while/body/eval_jaxpr/ppermute | solution.py:29
  206.4 8.0 collective-permute-start
  213.2 3.3 collective-permute-start.1
  217.3 10.2 %collective-permute-start.2 = (bf16[8,8,8,512]{3,2,1,0:T(8,128)(2,1)S(1)}, bf16[8,8,8,512]{3,2,1,0:T(8,128)(2,1)S(1)}, u32[]{:S(2)}, u32[]{:S(2)}) collective-permute-start(bf16[8,8,8,512]{3,2,1,0:T(8,128)(2,1)S(1)} %get-tuple-element.522), channel_id=1, source_target_pairs={{0,32},{32,64},{64,96},{96,128},{128,160},{160,192},{192,224},{1,3... | collective-permute-start | bytes 1572872 | tf_op jit(solution)/shard_map/while/body/eval_jaxpr/ppermute | solution.py:29
  230.1 8.0 collective-permute-start
  236.9 3.3 collective-permute-start.1
  241.0 16.8 %collective-permute-start.2 = (bf16[8,8,8,512]{3,2,1,0:T(8,128)(2,1)S(1)}, bf16[8,8,8,512]{3,2,1,0:T(8,128)(2,1)S(1)}, u32[]{:S(2)}, u32[]{:S(2)}) collective-permute-start(bf16[8,8,8,512]{3,2,1,0:T(8,128)(2,1)S(1)} %get-tuple-element.522), channel_id=1, source_target_pairs={{0,32},{32,64},{64,96},{96,128},{128,160},{160,192},{192,224},{1,3... | collective-permute-start | bytes 1572872 | tf_op jit(solution)/shard_map/while/body/eval_jaxpr/ppermute | solution.py:29
  262.3 8.2 %collective-permute-start.3 = (bf16[8,8,4,512]{3,2,1,0:T(4,128)(2,1)}, bf16[8,8,4,512]{3,2,1,0:T(4,128)(2,1)}, u32[]{:S(2)}, u32[]{:S(2)}) collective-permute-start(bf16[8,8,4,512]{3,2,1,0:T(4,128)(2,1)} %get-tuple-element.439), channel_id=1, source_target_pairs={{1,0},{2,1},{3,2},{4,3},{5,4},{6,5},{7,6},{8,7},{9,8},{10,9},{11,1... | collective-permute-start | bytes 786440 | tf_op jit(solution)/shard_map/while/body/eval_jaxpr/ppermute | solution.py:19
  269.1 3.3 collective-permute-start.4
  274.2 11.8 %collective-permute-start.5 = (bf16[8,8,8,512]{3,2,1,0:T(8,128)(2,1)S(1)}, bf16[8,8,8,512]{3,2,1,0:T(8,128)(2,1)}, u32[]{:S(2)}, u32[]{:S(2)}) collective-permute-start(bf16[8,8,8,512]{3,2,1,0:T(8,128)(2,1)S(1)} %get-tuple-element.523), channel_id=1, source_target_pairs={{32,0},{64,32},{96,64},{128,96},{160,128},{192,160},{224,192},{33,... | collective-permute-start | bytes 1572872 | tf_op jit(solution)/shard_map/while/body/eval_jaxpr/ppermute | solution.py:29
  289.5 8.3 %collective-permute-start.3 = (bf16[8,8,4,512]{3,2,1,0:T(4,128)(2,1)}, bf16[8,8,4,512]{3,2,1,0:T(4,128)(2,1)}, u32[]{:S(2)}, u32[]{:S(2)}) collective-permute-start(bf16[8,8,4,512]{3,2,1,0:T(4,128)(2,1)} %get-tuple-element.439), channel_id=1, source_target_pairs={{1,0},{2,1},{3,2},{4,3},{5,4},{6,5},{7,6},{8,7},{9,8},{10,9},{11,1... | collective-permute-start | bytes 786440 | tf_op jit(solution)/shard_map/while/body/eval_jaxpr/ppermute | solution.py:19
  296.3 3.3 collective-permute-start.4
  301.4 13.6 %collective-permute-start.5 = (bf16[8,8,8,512]{3,2,1,0:T(8,128)(2,1)S(1)}, bf16[8,8,8,512]{3,2,1,0:T(8,128)(2,1)}, u32[]{:S(2)}, u32[]{:S(2)}) collective-permute-start(bf16[8,8,8,512]{3,2,1,0:T(8,128)(2,1)S(1)} %get-tuple-element.523), channel_id=1, source_target_pairs={{32,0},{64,32},{96,64},{128,96},{160,128},{192,160},{224,192},{33,... | collective-permute-start | bytes 1572872 | tf_op jit(solution)/shard_map/while/body/eval_jaxpr/ppermute | solution.py:29
  318.5 8.3 %collective-permute-start.3 = (bf16[8,8,4,512]{3,2,1,0:T(4,128)(2,1)}, bf16[8,8,4,512]{3,2,1,0:T(4,128)(2,1)}, u32[]{:S(2)}, u32[]{:S(2)}) collective-permute-start(bf16[8,8,4,512]{3,2,1,0:T(4,128)(2,1)} %get-tuple-element.439), channel_id=1, source_target_pairs={{1,0},{2,1},{3,2},{4,3},{5,4},{6,5},{7,6},{8,7},{9,8},{10,9},{11,1... | collective-permute-start | bytes 786440 | tf_op jit(solution)/shard_map/while/body/eval_jaxpr/ppermute | solution.py:19
  325.3 3.3 collective-permute-start.4
  330.3 12.0 %collective-permute-start.5 = (bf16[8,8,8,512]{3,2,1,0:T(8,128)(2,1)S(1)}, bf16[8,8,8,512]{3,2,1,0:T(8,128)(2,1)}, u32[]{:S(2)}, u32[]{:S(2)}) collective-permute-start(bf16[8,8,8,512]{3,2,1,0:T(8,128)(2,1)S(1)} %get-tuple-element.523), channel_id=1, source_target_pairs={{32,0},{64,32},{96,64},{128,96},{160,128},{192,160},{224,192},{33,... | collective-permute-start | bytes 1572872 | tf_op jit(solution)/shard_map/while/body/eval_jaxpr/ppermute | solution.py:29
  345.9 8.3 %collective-permute-start.3 = (bf16[8,8,4,512]{3,2,1,0:T(4,128)(2,1)}, bf16[8,8,4,512]{3,2,1,0:T(4,128)(2,1)}, u32[]{:S(2)}, u32[]{:S(2)}) collective-permute-start(bf16[8,8,4,512]{3,2,1,0:T(4,128)(2,1)} %get-tuple-element.439), channel_id=1, source_target_pairs={{1,0},{2,1},{3,2},{4,3},{5,4},{6,5},{7,6},{8,7},{9,8},{10,9},{11,1... | collective-permute-start | bytes 786440 | tf_op jit(solution)/shard_map/while/body/eval_jaxpr/ppermute | solution.py:19
  352.7 3.3 collective-permute-start.4
  357.8 13.6 %collective-permute-start.5 = (bf16[8,8,8,512]{3,2,1,0:T(8,128)(2,1)S(1)}, bf16[8,8,8,512]{3,2,1,0:T(8,128)(2,1)}, u32[]{:S(2)}, u32[]{:S(2)}) collective-permute-start(bf16[8,8,8,512]{3,2,1,0:T(8,128)(2,1)S(1)} %get-tuple-element.523), channel_id=1, source_target_pairs={{32,0},{64,32},{96,64},{128,96},{160,128},{192,160},{224,192},{33,... | collective-permute-start | bytes 1572872 | tf_op jit(solution)/shard_map/while/body/eval_jaxpr/ppermute | solution.py:29
  374.9 8.3 %collective-permute-start.3 = (bf16[8,8,4,512]{3,2,1,0:T(4,128)(2,1)}, bf16[8,8,4,512]{3,2,1,0:T(4,128)(2,1)}, u32[]{:S(2)}, u32[]{:S(2)}) collective-permute-start(bf16[8,8,4,512]{3,2,1,0:T(4,128)(2,1)} %get-tuple-element.439), channel_id=1, source_target_pairs={{1,0},{2,1},{3,2},{4,3},{5,4},{6,5},{7,6},{8,7},{9,8},{10,9},{11,1... | collective-permute-start | bytes 786440 | tf_op jit(solution)/shard_map/while/body/eval_jaxpr/ppermute | solution.py:19
  381.6 3.3 collective-permute-start.4
  386.7 11.5 %collective-permute-start.5 = (bf16[8,8,8,512]{3,2,1,0:T(8,128)(2,1)S(1)}, bf16[8,8,8,512]{3,2,1,0:T(8,128)(2,1)}, u32[]{:S(2)}, u32[]{:S(2)}) collective-permute-start(bf16[8,8,8,512]{3,2,1,0:T(8,128)(2,1)S(1)} %get-tuple-element.523), channel_id=1, source_target_pairs={{32,0},{64,32},{96,64},{128,96},{160,128},{192,160},{224,192},{33,... | collective-permute-start | bytes 1572872 | tf_op jit(solution)/shard_map/while/body/eval_jaxpr/ppermute | solution.py:29
  401.8 8.3 %collective-permute-start.3 = (bf16[8,8,4,512]{3,2,1,0:T(4,128)(2,1)}, bf16[8,8,4,512]{3,2,1,0:T(4,128)(2,1)}, u32[]{:S(2)}, u32[]{:S(2)}) collective-permute-start(bf16[8,8,4,512]{3,2,1,0:T(4,128)(2,1)} %get-tuple-element.439), channel_id=1, source_target_pairs={{1,0},{2,1},{3,2},{4,3},{5,4},{6,5},{7,6},{8,7},{9,8},{10,9},{11,1... | collective-permute-start | bytes 786440 | tf_op jit(solution)/shard_map/while/body/eval_jaxpr/ppermute | solution.py:19
  408.6 3.3 collective-permute-start.4
  413.7 14.0 %collective-permute-start.5 = (bf16[8,8,8,512]{3,2,1,0:T(8,128)(2,1)S(1)}, bf16[8,8,8,512]{3,2,1,0:T(8,128)(2,1)}, u32[]{:S(2)}, u32[]{:S(2)}) collective-permute-start(bf16[8,8,8,512]{3,2,1,0:T(8,128)(2,1)S(1)} %get-tuple-element.523), channel_id=1, source_target_pairs={{32,0},{64,32},{96,64},{128,96},{160,128},{192,160},{224,192},{33,... | collective-permute-start | bytes 1572872 | tf_op jit(solution)/shard_map/while/body/eval_jaxpr/ppermute | solution.py:29
  431.3 8.3 %collective-permute-start.3 = (bf16[8,8,4,512]{3,2,1,0:T(4,128)(2,1)}, bf16[8,8,4,512]{3,2,1,0:T(4,128)(2,1)}, u32[]{:S(2)}, u32[]{:S(2)}) collective-permute-start(bf16[8,8,4,512]{3,2,1,0:T(4,128)(2,1)} %get-tuple-element.439), channel_id=1, source_target_pairs={{1,0},{2,1},{3,2},{4,3},{5,4},{6,5},{7,6},{8,7},{9,8},{10,9},{11,1... | collective-permute-start | bytes 786440 | tf_op jit(solution)/shard_map/while/body/eval_jaxpr/ppermute | solution.py:19
  438.0 3.3 collective-permute-start.4
  443.1 56.5 %collective-permute-start.5 = (bf16[8,8,8,512]{3,2,1,0:T(8,128)(2,1)S(1)}, bf16[8,8,8,512]{3,2,1,0:T(8,128)(2,1)}, u32[]{:S(2)}, u32[]{:S(2)}) collective-permute-start(bf16[8,8,8,512]{3,2,1,0:T(8,128)(2,1)S(1)} %get-tuple-element.523), channel_id=1, source_target_pairs={{32,0},{64,32},{96,64},{128,96},{160,128},{192,160},{224,192},{33,... | collective-permute-start | bytes 1572872 | tf_op jit(solution)/shard_map/while/body/eval_jaxpr/ppermute | solution.py:29
  503.1 8.3 %collective-permute-start.3 = (bf16[8,8,4,512]{3,2,1,0:T(4,128)(2,1)}, bf16[8,8,4,512]{3,2,1,0:T(4,128)(2,1)}, u32[]{:S(2)}, u32[]{:S(2)}) collective-permute-start(bf16[8,8,4,512]{3,2,1,0:T(4,128)(2,1)} %get-tuple-element.439), channel_id=1, source_target_pairs={{1,0},{2,1},{3,2},{4,3},{5,4},{6,5},{7,6},{8,7},{9,8},{10,9},{11,1... | collective-permute-start | bytes 786440 | tf_op jit(solution)/shard_map/while/body/eval_jaxpr/ppermute | solution.py:19
  509.9 3.3 collective-permute-start.4
  514.9 2.3 copy-start.2
  521.8 11.5 %collective-permute-start.5 = (bf16[8,8,8,512]{3,2,1,0:T(8,128)(2,1)S(1)}, bf16[8,8,8,512]{3,2,1,0:T(8,128)(2,1)}, u32[]{:S(2)}, u32[]{:S(2)}) collective-permute-start(bf16[8,8,8,512]{3,2,1,0:T(8,128)(2,1)S(1)} %get-tuple-element.523), channel_id=1, source_target_pairs={{32,0},{64,32},{96,64},{128,96},{160,128},{192,160},{224,192},{33,... | collective-permute-start | bytes 1572872 | tf_op jit(solution)/shard_map/while/body/eval_jaxpr/ppermute | solution.py:29
  536.8 8.3 %collective-permute-start.3 = (bf16[8,8,4,512]{3,2,1,0:T(4,128)(2,1)}, bf16[8,8,4,512]{3,2,1,0:T(4,128)(2,1)}, u32[]{:S(2)}, u32[]{:S(2)}) collective-permute-start(bf16[8,8,4,512]{3,2,1,0:T(4,128)(2,1)} %get-tuple-element.439), channel_id=1, source_target_pairs={{1,0},{2,1},{3,2},{4,3},{5,4},{6,5},{7,6},{8,7},{9,8},{10,9},{11,1... | collective-permute-start | bytes 786440 | tf_op jit(solution)/shard_map/while/body/eval_jaxpr/ppermute | solution.py:19
  543.6 3.3 collective-permute-start.4
  548.7 2.3 copy-start.2
  555.5 10.0 %collective-permute-start.5 = (bf16[8,8,8,512]{3,2,1,0:T(8,128)(2,1)S(1)}, bf16[8,8,8,512]{3,2,1,0:T(8,128)(2,1)}, u32[]{:S(2)}, u32[]{:S(2)}) collective-permute-start(bf16[8,8,8,512]{3,2,1,0:T(8,128)(2,1)S(1)} %get-tuple-element.523), channel_id=1, source_target_pairs={{32,0},{64,32},{96,64},{128,96},{160,128},{192,160},{224,192},{33,... | collective-permute-start | bytes 1572872 | tf_op jit(solution)/shard_map/while/body/eval_jaxpr/ppermute | solution.py:29
  565.5 1.2 copy-start.3
  718.5 76.4 %copy-start.5 = (f32[16,16]{1,0:T(8,128)}, f32[16,16]{1,0:T(8,128)S(1)}, u32[]{:S(2)}) copy-start(f32[16,16]{1,0:T(8,128)S(1)} %psum.30) | copy-start | bytes 3076
Sparse Core Ops, SparseCore 0:
  566.8 68.7 all-reduce.3
